TPU v7x, 256 devices: a whole 4x4x8 slice. The times are simulated.
256 devices in a mesh: replica: 4 (over z_hi, core), fsdp: 64 (over z_lo, x, y).
Axes of the slice: x: 4, y: 4, z: 8 (z_hi: 2, z_lo: 4; z = z_hi * 4 + z_lo), core: 2. Of those that a mesh axis runs over, the one named last changes fastest.
Arguments:
- tokens: bfloat16 [65536, 2048], P(('replica', 'fsdp')), may hold values from -6 to 6
- inner_q: bfloat16 [4, 2048, 2048], P('replica', 'fsdp')
- inner_k: bfloat16 [4, 2048, 512], P('replica', 'fsdp')
- inner_v: bfloat16 [4, 2048, 512], P('replica', 'fsdp')
- outer_q: float32 [2048, 2048], P('fsdp')
- outer_k: float32 [2048, 512], P('fsdp')
- outer_v: float32 [2048, 512], P('fsdp')
- moment_q: float32 [2048, 2048], P('fsdp', 'replica'), may hold values from -0.09375 to 0.09375
- moment_k: float32 [2048, 512], P('fsdp', 'replica'), may hold values from -0.09375 to 0.09375
- value_momentum: float32 [2048, 512], P('fsdp', 'replica'), may hold values from -0.09375 to 0.09375
Outputs:
- projected: bfloat16 [65536, 3072], P(('replica', 'fsdp'))
- updated_outer_query: float32 [2048, 2048], P('fsdp')
- updated_outer_key: float32 [2048, 512], P('fsdp')
- new_outer_v: float32 [2048, 512], P('fsdp')
- new_moment_q: float32 [2048, 2048], P('fsdp', 'replica')
- new_moment_k: float32 [2048, 512], P('fsdp', 'replica')
- new_moment_v: float32 [2048, 512], P('fsdp', 'replica')
All inputs are finite; a program needn't handle non-finite values.
Results may differ from a plain program's by a relative error of at most 0.005.
Values may be sent and summed in bfloat16 or wider, within the bound.
A program may use at most 64 MiB of HBM per device.

v0:
```python
import jax
import jax.numpy as jnp
from jax import lax
from jax.sharding import PartitionSpec as P

LEARN_RATE = 0.7
MOMENTUM_BETA = 0.9


def per_device(
    tokens, inner_q, inner_k, inner_v, outer_q, outer_k, outer_v, moment_q, moment_k, value_momentum
):
    worker_count = lax.axis_size("replica")
    worker_index = lax.axis_index("replica")
    outers = (outer_q, outer_k, outer_v)
    moments = (moment_q, moment_k, value_momentum)
    differences = tuple(
        (
            outer - inner[0].astype(jnp.float32)
            for outer, inner in zip(outers, (inner_q, inner_k, inner_v))
        )
    )
    summed = lax.psum_scatter(differences, "replica", scatter_dimension=1, tiled=True)
    owned_outer = []
    owned_moment = []
    for total, outer, outer_momentum in zip(summed, outers, moments):
        width = outer_momentum.shape[1]
        pseudo = total / worker_count
        new_moment = MOMENTUM_BETA * outer_momentum + pseudo
        own_slice = lax.dynamic_slice_in_dim(outer, worker_index * width, width, 1)
        owned_outer.append(own_slice - LEARN_RATE * (pseudo + MOMENTUM_BETA * new_moment))
        owned_moment.append(new_moment)
    full_outer = lax.all_gather(tuple(owned_outer), "replica", axis=1, tiled=True)
    local_fresh = jnp.concatenate([weight.astype(jnp.bfloat16) for weight in full_outer], axis=1)
    fresh = lax.all_gather(local_fresh, "fsdp", axis=0, tiled=True)
    projected = jnp.dot(tokens, fresh, preferred_element_type=jnp.float32).astype(jnp.bfloat16)
    return (
        projected,
        full_outer[0],
        full_outer[1],
        full_outer[2],
        owned_moment[0],
        owned_moment[1],
        owned_moment[2],
    )


def solution(mesh):
    placed = (
        P(("replica", "fsdp"), None),
        P("replica", "fsdp", None),
        P("replica", "fsdp", None),
        P("replica", "fsdp", None),
        P("fsdp", None),
        P("fsdp", None),
        P("fsdp", None),
        P("fsdp", "replica"),
        P("fsdp", "replica"),
        P("fsdp", "replica"),
    )
    return jax.shard_map(
        per_device,
        mesh=mesh,
        in_specs=placed,
        out_specs=(
            P(("replica", "fsdp"), None),
            P("fsdp", None),
            P("fsdp", None),
            P("fsdp", None),
            P("fsdp", "replica"),
            P("fsdp", "replica"),
            P("fsdp", "replica"),
        ),
        check_vma=False,
    )
```

profile of v0, /device:TPU:16, one launch (start us, length us, event | category | flops | bytes accessed | tf_op | source)
XLA Modules:
  0.0 515.0 jit_solution(6536881610488813657)
XLA Ops:
  7.2 0.0 copy-start
  7.2 0.0 reduce-scatter.6.cloned.1.call-start
  7.2 1.6 convert_subtract_fusion.2
  8.8 0.0 reduce-scatter.6.cloned.1.call-update
  8.8 0.0 reduce-scatter.8.cloned.1.call-start
  8.9 1.5 convert_subtract_fusion.1
  10.3 0.0 reduce-scatter.8.cloned.1.call-update
  10.4 0.0 reduce-scatter.4.cloned.1.call-start
  10.4 1.7 convert_subtract_fusion
  12.1 0.0 reduce-scatter.4.cloned.1.call-update
  12.2 0.0 all-gather.2.cloned.1.call-start
  12.2 36.2 %reduce-scatter.6.cloned.1.call-done = f32[32,128]{1,0:T(8,128)} async-done(((f32[32,512]{1,0:T(8,128)}), f32[32,128]{1,0:T(8,128)}) %reduce-scatter.6.cloned.1.call-update) | async-done | bytes 16400 | tf_op jit(solution)/shard_map/reduce_scatter | solution.py:23
  48.4 1.4 multiply_subtract_fusion.2
  49.8 9.1 %all_gather.13 = f32[32,512]{1,0:T(8,128)S(1)} all-gather(f32[32,128]{1,0:T(8,128)S(1)} %get-tuple-element.16), channel_id=1, replica_groups=mesh['replica'=4,'fsdp'=64] {'replica'}, dimensions={1}, use_global_device_ids=true | all-gather | bytes 81920 | tf_op jit(solution)/shard_map/all_gather | solution.py:33
  58.9 23.6 %reduce-scatter.8.cloned.1.call-done = f32[32,128]{1,0:T(8,128)} async-done(((f32[32,512]{1,0:T(8,128)}), f32[32,128]{1,0:T(8,128)}) %reduce-scatter.8.cloned.1.call-update) | async-done | bytes 16400 | tf_op jit(solution)/shard_map/reduce_scatter | solution.py:23
  82.5 1.4 multiply_subtract_fusion.1
  83.9 9.1 %all_gather.14 = f32[32,512]{1,0:T(8,128)S(1)} all-gather(f32[32,128]{1,0:T(8,128)S(1)} %get-tuple-element.18), channel_id=1, replica_groups=mesh['replica'=4,'fsdp'=64] {'replica'}, dimensions={1}, use_global_device_ids=true | all-gather | bytes 81920 | tf_op jit(solution)/shard_map/all_gather | solution.py:33
  93.0 25.5 %reduce-scatter.4.cloned.1.call-done = f32[32,512]{1,0:T(8,128)} async-done(((f32[32,2048]{1,0:T(8,128)}), f32[32,512]{1,0:T(8,128)}) %reduce-scatter.4.cloned.1.call-update) | async-done | bytes 65552 | tf_op jit(solution)/shard_map/reduce_scatter | solution.py:23
  118.5 1.5 multiply_subtract_fusion
  120.1 9.7 %all_gather.12 = f32[32,2048]{1,0:T(8,128)S(1)} all-gather(f32[32,512]{1,0:T(8,128)S(1)} %get-tuple-element.14), channel_id=1, replica_groups=mesh['replica'=4,'fsdp'=64] {'replica'}, dimensions={1}, use_global_device_ids=true | all-gather | bytes 327680 | tf_op jit(solution)/shard_map/all_gather | solution.py:33
  129.8 0.7 pad_maximum_fusion
  130.5 0.0 all-gather.2.cloned.1.call-update
  130.5 365.9 %all-gather.2.cloned.1.call-done = bf16[2048,3072]{1,0:T(8,128)(2,1)} async-done(((bf16[32,3072]{1,0:T(8,128)(2,1)}), bf16[2048,3072]{1,0:T(8,128)(2,1)}) %all-gather.2.cloned.1.call-update) | async-done | bytes 12582928 | tf_op jit(solution)/shard_map/all_gather | solution.py:35
  496.4 0.0 copy-done
  496.4 8.3 %fusion = bf16[256,3072]{0,1:T(8,128)(2,1)S(1)} fusion(bf16[2048,3072]{1,0:T(8,128)(2,1)} %all-gather.2.cloned.1.call-done, bf16[256,2048]{1,0:T(8,128)(2,1)S(1)} %copy-done), kind=kOutput, calls=%fused_computation.1 | convolution fusion | flops 3222011904 | bytes 15204352 | tf_op jit(solution)/shard_map/dot_general | solution.py:36
  504.7 1.7 copy.17
  506.5 0.7 copy.21
  507.2 0.6 copy.22
  507.8 0.6 copy.23
  (3 shorter events, 0.0 us)
Async XLA Ops:
  7.2 489.2 %copy-start = (bf16[256,2048]{1,0:T(8,128)(2,1)S(1)}, bf16[256,2048]{1,0:T(8,128)(2,1)}, u32[]{:S(2)}) copy-start(bf16[256,2048]{1,0:T(8,128)(2,1)} %param.10) | copy-start | bytes 3145732
  7.2 41.2 %reduce-scatter.6.cloned.1.call-start = ((), (), s32[]{:S(2)}) async-start(), calls=%async_computation.4 | async-start | bytes 81920 | tf_op jit(solution)/shard_map/reduce_scatter | solution.py:23
  8.8 73.7 %reduce-scatter.8.cloned.1.call-start = ((), (), s32[]{:S(2)}) async-start(), calls=%async_computation.5 | async-start | bytes 81920 | tf_op jit(solution)/shard_map/reduce_scatter | solution.py:23
  10.4 108.2 %reduce-scatter.4.cloned.1.call-start = ((), (), s32[]{:S(2)}) async-start(), calls=%async_computation.3 | async-start | bytes 327680 | tf_op jit(solution)/shard_map/reduce_scatter | solution.py:23
  12.2 484.3 %all-gather.2.cloned.1.call-start = ((), (), s32[]{:S(2)}) async-start(), calls=%async_computation.6 | async-start | bytes 12779520 | tf_op jit(solution)/shard_map/all_gather | solution.py:35
Sparse Core Ops, SparseCore 0:
  11.2 37.1 reduce-scatter.5
  51.6 30.8 reduce-scatter.7
  85.8 32.7 reduce-scatter.3
  130.6 365.7 all-gather.1
where the time goes:
time: 515 us
  waiting for transfers between devices  451 us (88%)
  blocking collectives  27.9 us (5%)
  between operations  13.8 us (3%)
  other arithmetic  9.75 us (2%)
  matrix products  8.3 us (2%)
    all_gather x1, waiting for transfers between devices, per_device(): fresh = lax.all_gather(local_fresh, 'fsdp', axis=0, tiled=True)  366 us
    reduce_scatter x3, waiting for transfers between devices, per_device(): lax.psum_scatter(differences, 'replica', scatter_dimension=1, tiled=True)  85.3 us
    all_gather x3, blocking collectives, per_device(): lax.all_gather(tuple(owned_outer), 'replica', axis=1, tiled=True)  27.9 us
  transfers between devices with their start and end apart: 4, of which 4 were waited for; matrix products, arithmetic and copies ran while one was open for 1% of the time, Pallas kernels for 0%

commit v1 on v0

--- a/solution.py
+++ b/solution.py
@@ -1,3 +1,4 @@
+import functools
 import jax
 import jax.numpy as jnp
 from jax import lax
@@ -5,6 +6,19 @@
 
 LEARN_RATE = 0.7
 MOMENTUM_BETA = 0.9
+
+
+def plan_case_for(shard_in, shard_axis):
+    seen_now = lax.all_to_all(
+        jnp.stack([shard_in] * lax.axis_size(shard_axis), 0),
+        axis_name=shard_axis,
+        split_axis=0,
+        concat_axis=0,
+    )
+    return jnp.concatenate(seen_now, axis=0)
+
+
+return_all_field = functools.partial(plan_case_for, shard_axis="fsdp")
 
 
 def per_device(
@@ -32,7 +46,7 @@
         owned_moment.append(new_moment)
     full_outer = lax.all_gather(tuple(owned_outer), "replica", axis=1, tiled=True)
     local_fresh = jnp.concatenate([weight.astype(jnp.bfloat16) for weight in full_outer], axis=1)
-    fresh = lax.all_gather(local_fresh, "fsdp", axis=0, tiled=True)
+    fresh = return_all_field(local_fresh)
     projected = jnp.dot(tokens, fresh, preferred_element_type=jnp.float32).astype(jnp.bfloat16)
     return (
         projected,

time: 515 us -> 434 us (0.84)
  waiting for transfers between devices: 451 us -> 85.4 us
  blocking collectives: 27.9 us -> 311 us
  local copies, waits for them, and re-layouts: 3.71 us -> 9.85 us
    all_gather x1 -> x0, waiting for transfers between devices: 366 us -> none  [per_device(): fresh = lax.all_gather(local_fresh, 'fsdp', axis=0, tiled=True)]
    all_to_all x0 -> x1, blocking collectives: none -> 283 us  [plan_case_for(): lax.all_to_all(jnp.stack([shard_in] * lax.axis_size(shard_axis), 0), axis...]
    another operation x0 -> x1, local copies, waits for them, and re-layouts: none -> 6.14 us  [plan_case_for(): jnp.stack([shard_in] * lax.axis_size(shard_axis), 0)]
  transfers between devices with their start and end apart: 4 -> 3, of which waited for: 4 -> 3; matrix products, arithmetic and copies ran while one was open for 1% -> 1% of each run, Pallas kernels for 0% -> 0%
where the time goes in v1:
time: 434 us
  blocking collectives  311 us (72%)
  waiting for transfers between devices  85.4 us (20%)
  between operations  13.8 us (3%)
  local copies, waits for them, and re-layouts  9.85 us (2%)
  other arithmetic  9.07 us (2%)
    all_to_all x1, blocking collectives, plan_case_for(): lax.all_to_all(jnp.stack([shard_in] * lax.axis_size(shard_axis), 0), axis...  283 us
    reduce_scatter x3, waiting for transfers between devices, per_device(): lax.psum_scatter(differences, 'replica', scatter_dimension=1, tiled=True)  85.4 us
    all_gather x3, blocking collectives, per_device(): lax.all_gather(tuple(owned_outer), 'replica', axis=1, tiled=True)  27.9 us
  transfers between devices with their start and end apart: 3, of which 3 were waited for; matrix products, arithmetic and copies ran while one was open for 1% of the time, Pallas kernels for 0%

profile of v1, /device:TPU:16, one launch (start us, length us, event | category | flops | bytes accessed | tf_op | source)
XLA Modules:
  0.0 433.5 jit_solution(16940068154737034783)
XLA Ops:
  7.2 0.0 copy-start
  7.2 0.0 reduce-scatter.6.cloned.1.call-start
  7.2 1.6 convert_subtract_fusion.2
  8.8 0.0 reduce-scatter.6.cloned.1.call-update
  8.8 0.0 reduce-scatter.8.cloned.1.call-start
  8.9 1.5 convert_subtract_fusion.1
  10.3 0.0 reduce-scatter.8.cloned.1.call-update
  10.4 0.0 reduce-scatter.4.cloned.1.call-start
  10.4 1.7 convert_subtract_fusion
  12.1 0.0 reduce-scatter.4.cloned.1.call-update
  12.2 36.2 %reduce-scatter.6.cloned.1.call-done = f32[32,128]{1,0:T(8,128)} async-done(((f32[32,512]{1,0:T(8,128)}), f32[32,128]{1,0:T(8,128)}) %reduce-scatter.6.cloned.1.call-update) | async-done | bytes 16400 | tf_op jit(solution)/shard_map/reduce_scatter | solution.py:37
  48.4 1.4 multiply_subtract_fusion.2
  49.8 9.1 %all_gather.10 = f32[32,512]{1,0:T(8,128)S(1)} all-gather(f32[32,128]{1,0:T(8,128)S(1)} %get-tuple-element.16), channel_id=1, replica_groups=mesh['replica'=4,'fsdp'=64] {'replica'}, dimensions={1}, use_global_device_ids=true | all-gather | bytes 81920 | tf_op jit(solution)/shard_map/all_gather | solution.py:47
  58.9 23.6 %reduce-scatter.8.cloned.1.call-done = f32[32,128]{1,0:T(8,128)} async-done(((f32[32,512]{1,0:T(8,128)}), f32[32,128]{1,0:T(8,128)}) %reduce-scatter.8.cloned.1.call-update) | async-done | bytes 16400 | tf_op jit(solution)/shard_map/reduce_scatter | solution.py:37
  82.5 1.4 multiply_subtract_fusion.1
  83.9 9.1 %all_gather.11 = f32[32,512]{1,0:T(8,128)S(1)} all-gather(f32[32,128]{1,0:T(8,128)S(1)} %get-tuple-element.18), channel_id=1, replica_groups=mesh['replica'=4,'fsdp'=64] {'replica'}, dimensions={1}, use_global_device_ids=true | all-gather | bytes 81920 | tf_op jit(solution)/shard_map/all_gather | solution.py:47
  93.0 25.5 %reduce-scatter.4.cloned.1.call-done = f32[32,512]{1,0:T(8,128)} async-done(((f32[32,2048]{1,0:T(8,128)}), f32[32,512]{1,0:T(8,128)}) %reduce-scatter.4.cloned.1.call-update) | async-done | bytes 65552 | tf_op jit(solution)/shard_map/reduce_scatter | solution.py:37
  118.5 1.5 multiply_subtract_fusion
  120.1 9.7 %all_gather.9 = f32[32,2048]{1,0:T(8,128)S(1)} all-gather(f32[32,512]{1,0:T(8,128)S(1)} %get-tuple-element.14), channel_id=1, replica_groups=mesh['replica'=4,'fsdp'=64] {'replica'}, dimensions={1}, use_global_device_ids=true | all-gather | bytes 327680 | tf_op jit(solution)/shard_map/all_gather | solution.py:47
  129.8 6.1 %stack.2 = bf16[64,32,3072]{2,1,0:T(8,128)(2,1)} broadcast(bf16[32,3072]{1,0:T(8,128)(2,1)S(1)} %pad_maximum_fusion), dimensions={1,2} | broadcast | bytes 12779520 | tf_op jit(solution)/shard_map/stack | solution.py:13
  136.0 283.3 %all_to_all.5 = bf16[64,32,3072]{2,1,0:T(8,128)(2,1)S(1)} all-to-all(bf16[64,32,3072]{2,1,0:T(8,128)(2,1)} %stack.2), channel_id=1, replica_groups=mesh['replica'=4,'fsdp'=64] {'fsdp'}, dimensions={0} | all-to-all | bytes 25165824 | tf_op jit(solution)/shard_map/all_to_all | solution.py:12
  419.3 0.0 copy-done
  419.3 4.0 fusion
  423.3 1.7 copy.17
  425.1 0.7 copy.21
  425.8 0.6 copy.22
  426.4 0.6 copy.23
  (4 shorter events, 0.0 us)
Async XLA Ops:
  7.2 412.1 %copy-start = (bf16[256,2048]{1,0:T(8,128)(2,1)S(1)}, bf16[256,2048]{1,0:T(8,128)(2,1)}, u32[]{:S(2)}) copy-start(bf16[256,2048]{1,0:T(8,128)(2,1)} %param.10) | copy-start | bytes 3145732
  7.2 41.2 %reduce-scatter.6.cloned.1.call-start = ((), (), s32[]{:S(2)}) async-start(), calls=%async_computation.5 | async-start | bytes 81920 | tf_op jit(solution)/shard_map/reduce_scatter | solution.py:37
  8.8 73.7 %reduce-scatter.8.cloned.1.call-start = ((), (), s32[]{:S(2)}) async-start(), calls=%async_computation.6 | async-start | bytes 81920 | tf_op jit(solution)/shard_map/reduce_scatter | solution.py:37
  10.4 108.2 %reduce-scatter.4.cloned.1.call-start = ((), (), s32[]{:S(2)}) async-start(), calls=%async_computation.4 | async-start | bytes 327680 | tf_op jit(solution)/shard_map/reduce_scatter | solution.py:37
Sparse Core Ops, SparseCore 0:
  11.2 37.1 reduce-scatter.5
  51.6 30.8 reduce-scatter.7
  85.8 32.7 reduce-scatter.3
